TPU v7x, 32 devices: a whole 2x2x4 slice. The times are simulated.
32 devices in a mesh: row: 2 (over y), col: 16 (over z, x, core).
Axes of the slice: x: 2, y: 2, z: 4, core: 2. Of those that a mesh axis runs over, the one named last changes fastest.
Arguments:
- eigen_slab: float32 [2048, 16384], P('row', 'col'), may hold values from -6 to 6
- secular_poles: float32 [32768], P('col'), may hold values from 0 to 4, as said below
- coupling: float32 [32768], P('col'), may hold values from -7 to 7
- window_roots: float32 [128], replicated, may hold values from 0 to 4, as said below
- deflated: int32 [32768], P('col'), may hold values 0 or 1
- column_map: int32 [32768], P('col'), may hold values from 0 to 32767, as said below
Outputs:
- vectors: float32 [2048, 128], P(('row', 'col'))
Inputs may be any that keep to these rules, and one draw needn't show every extreme that they name: `column_map`: A permutation of the 32768 columns. Grid column c holds columns c * 1024 to (c + 1) * 1024 - 1 and 16384 + c * 1024 to 16384 + (c + 1) * 1024 - 1 of the slab, and positions c * 2048 to (c + 1) * 2048 - 1. Of one grid column's positions, exactly 256 map to the columns of one grid column, 128 to each of 14 others, none to the remaining one. `secular_poles`: each pole lies between (k + 0.2) * 4 / 64 and (k + 0.8) * 4 / 64 for a whole number k. `window_roots`: each root lies within 0.15 * 4 / 64 of k * 4 / 64 for a whole number k of 1 to 63.
All inputs are finite; a program needn't handle non-finite values. No bound on the sum of `deflated` on one device may be relied on, other than what follows from the above.
Results may differ from a plain program's by a relative error of at most 0.0003.
Values sent between devices are 32-bit elements; how exact they have to be, the bound alone decides.
No kernel may reach another device: no remote copies, remote signals or barrier semaphores. Data moves between devices by JAX's collectives and lax.ppermute only.
A program may use at most 64 MiB of HBM per device.

v0:
```python
import jax
import jax.numpy as jnp
from jax import lax
from jax.sharding import PartitionSpec as P


def slot_plan(column_map, groups, cols_dev, capacity):
    block_len = column_map.shape[0]
    half_order = cols_dev * groups
    within = column_map % half_order
    target = within // cols_dev
    target_local = within % cols_dev + jnp.where(column_map >= half_order, cols_dev, 0)
    onehot = (target[:, None] == jnp.arange(groups, dtype=jnp.int32)[None, :]).astype(jnp.int32)
    slot_rank = jnp.sum(jnp.cumsum(onehot, axis=0) * onehot, axis=1) - 1
    slot_index = target * capacity + slot_rank
    sentinel = jnp.full((groups * capacity,), block_len, jnp.int32)
    slot_source = sentinel.at[slot_index].set(jnp.arange(block_len, dtype=jnp.int32))
    slot_target = sentinel.at[slot_index].set(target_local)
    return (slot_source, slot_target)


def route_generators(
    coupling, secular_poles, deflated, column_map, chosen_roots, inverse, groups, cols_dev, capacity
):
    block_len = column_map.shape[0]
    slot_source, slot_target = slot_plan(column_map, groups, cols_dev, capacity)
    live_coupling = jnp.where(deflated == 0, coupling, jnp.zeros_like(coupling))
    out_coupling = jnp.take(live_coupling, slot_source, mode="fill", fill_value=0.0).reshape(
        groups, capacity
    )
    out_poles = jnp.take(secular_poles, slot_source, mode="fill", fill_value=0.0).reshape(
        groups, capacity
    )
    got_coupling, got_poles, got_index = (
        lax.all_to_all(out_coupling, "col", split_axis=0, concat_axis=0, tiled=True),
        lax.all_to_all(out_poles, "col", split_axis=0, concat_axis=0, tiled=True),
        lax.all_to_all(
            slot_target.reshape(groups, capacity), "col", split_axis=0, concat_axis=0, tiled=True
        ),
    )
    distance = got_poles.reshape(-1)[:, None] - chosen_roots[None, :]
    rebuilt = got_coupling.reshape(-1)[:, None] / distance * inverse[None, :]
    empty = jnp.zeros((block_len, chosen_roots.shape[0]), jnp.float32)
    return empty.at[got_index.reshape(-1)].set(rebuilt, mode="drop")


def body(eigen_slab, secular_poles, coupling, window_roots, deflated, column_map):
    groups = lax.axis_size("col")
    row_groups = lax.axis_size("row")
    block_len = secular_poles.shape[0]
    cols_dev = eigen_slab.shape[1]
    capacity = 2 * (block_len // groups)
    distance = secular_poles[:, None] - window_roots[None, :]
    entries = jnp.where(
        deflated[:, None] == 0, coupling[:, None] / distance, jnp.zeros_like(distance)
    )
    sum_squares = lax.psum(jnp.sum(entries * entries, axis=0), "col")
    inverse = lax.rsqrt(sum_squares)
    placed = route_generators(
        coupling,
        secular_poles,
        deflated,
        column_map,
        window_roots,
        inverse,
        groups,
        cols_dev,
        capacity,
    )
    half_start = jnp.where(lax.axis_index("row") < row_groups // 2, 0, cols_dev)
    half_window = lax.dynamic_slice_in_dim(placed, half_start, cols_dev, 0)
    return lax.psum_scatter(
        jnp.dot(
            eigen_slab,
            half_window,
            precision=lax.Precision.HIGHEST,
            preferred_element_type=jnp.float32,
        ),
        "col",
        scatter_dimension=0,
        tiled=True,
    )


def solution(mesh):
    return jax.shard_map(
        body,
        mesh=mesh,
        in_specs=(P("row", "col"), P("col"), P("col"), P(), P("col"), P("col")),
        out_specs=P(("row", "col"), None),
        check_vma=False,
    )
```

profile of v0, /device:TPU:0, one launch (start us, length us, event | category | flops | bytes accessed | tf_op | source)
XLA Modules:
  0.0 217.3 jit_solution(6445857893102365710)
XLA Ops:
  6.5 0.7 fusion.15
  7.3 4.5 %reduce-window.6 = s32[16,16,128]{2,1,0:T(8,128)S(1)} reduce-window(s32[16,16,128]{2,1,0:T(8,128)S(1)} %fusion.12, s32[]{:T(128)} %constant.67.clone.1), window={size=1x1x128 pad=0_0x0_0x127_0}, to_apply=%region_0.1 | reduce-window | flops 4161536 | bytes 262148 | tf_op jit(solution)/shard_map/reduce-window
  11.8 0.4 slice_reduce_fusion
  12.3 0.2 reduce-window.9
  12.4 0.1 broadcast_add_fusion
  12.5 0.1 fusion.11
  12.6 8.6 %scatter_custom_fusion = s32[4096]{0:T(1024)} fusion(s32[2048]{0:T(1024)S(1)} %compare_select_fusion.2, s32[2048]{0:T(1024)S(1)} %get-tuple-element.10, s32[]{:T(128)} %constant.66.clone.1), kind=kCustom, calls=%fused_computation.45 | custom fusion | bytes 16388 | tf_op jit(solution)/shard_map/scatter | solution.py:18
  21.2 7.4 %all-to-all-start = ((s32[16,1,256]{2,1,0:T(1,128)}), s32[16,1,256]{2,1,0:T(1,128)S(1)}, u32[]{:S(2)}, u32[]{:S(2)}) async-start(s32[16,1,256]{2,1,0:T(1,128)} %bitcast.2), calls=%async_computation | async-start | bytes 32768 | tf_op jit(solution)/shard_map/all_to_all | solution.py:37
  28.6 8.1 %scatter_custom_fusion.1 = s32[4096]{0:T(1024)S(1)} fusion(s32[2048]{0:T(1024)S(1)} %compare_select_fusion.2, s32[2048]{0:T(1024)S(1)} %iota.11, s32[]{:T(128)} %constant.66.clone.1), kind=kCustom, calls=%fused_computation.43 | custom fusion | bytes 16388 | tf_op jit(solution)/shard_map/scatter | solution.py:17
  36.7 0.7 broadcast_select_fusion.2
  37.4 23.0 %gather_fusion = f32[4096]{0:T(1024)S(1)} fusion(f32[2048]{0:T(1024)S(1)} %get-tuple-element.8, s32[4096]{0:T(1024)S(1)} %fusion.13), kind=kCustom, calls=%fused_computation.clone | custom fusion | bytes 49152 | tf_op jit(solution)/shard_map/jit(_take)/gather | solution.py:28
  60.5 0.0 copy-start
  60.5 0.6 broadcast_select_fusion.1
  61.1 0.1 copy-done
  61.2 0.0 copy-start.1
  61.2 23.0 %gather_fusion.1 = f32[4096]{0:T(1024)S(1)} fusion(f32[2048]{0:T(1024)S(1)} %copy-done, s32[4096]{0:T(1024)S(1)} %fusion.13), kind=kCustom, calls=%fused_computation.1.clone | custom fusion | bytes 49152 | tf_op jit(solution)/shard_map/jit(_take)/gather | solution.py:31
  84.2 0.6 broadcast_select_fusion
  84.8 0.0 all-to-all-done
  84.8 6.0 %all-to-all-start.2 = ((f32[16,1,256]{2,1,0:T(1,128)}), f32[16,1,256]{2,1,0:T(1,128)S(1)}, u32[]{:S(2)}, u32[]{:S(2)}) async-start(f32[16,1,256]{2,1,0:T(1,128)} %bitcast.7), calls=%async_computation.2 | async-start | bytes 32768 | tf_op jit(solution)/shard_map/all_to_all | solution.py:36
  90.8 0.0 copy-done.1
  90.9 0.0 copy-done.2
  90.9 1.0 multiply_reduce_fusion
  91.9 33.8 %psum.7 = f32[128]{0:T(128)S(1)} all-reduce(f32[128]{0:T(128)S(1)} %multiply_reduce_fusion), channel_id=1, replica_groups=mesh['row'=2,'col'=16] {'col'}, use_global_device_ids=true, to_apply=%region_6.8 | all-reduce | flops 128 | bytes 1024 | tf_op jit(solution)/shard_map/psum | solution.py:57
  125.7 0.0 all-to-all-done.2
  125.7 3.5 %all-to-all-start.1 = ((f32[16,1,256]{2,1,0:T(1,128)}), f32[16,1,256]{2,1,0:T(1,128)S(1)}, u32[]{:S(2)}, u32[]{:S(2)}) async-start(f32[16,1,256]{2,1,0:T(1,128)} %bitcast.5), calls=%async_computation.1 | async-start | bytes 32768 | tf_op jit(solution)/shard_map/all_to_all | solution.py:35
  129.2 0.0 reduce-scatter.4.cloned.1.call-start
  129.3 6.4 %all-to-all-done.1 = f32[16,1,256]{2,1,0:T(1,128)S(1)} async-done(((f32[16,1,256]{2,1,0:T(1,128)}), f32[16,1,256]{2,1,0:T(1,128)S(1)}, u32[]{:S(2)}, u32[]{:S(2)}) %all-to-all-start.1) | async-done | bytes 16416 | tf_op jit(solution)/shard_map/all_to_all | solution.py:35
  135.7 13.5 %scatter_custom_fusion.2 = f32[2048,128]{1,0:T(8,128)S(1)} fusion(s32[4096]{0:T(1024)S(1)} %bitcast.35, f32[128]{0:T(128)S(1)} %rsqrt.3, f32[128]{0:T(128)S(1)} %copy-done.2, f32[4096]{0:T(1024)S(1)} %bitcast.31, f32[4096]{0:T(1024)S(1)} %bitcast.32, f32[]{:T(128)} %constant.65.clone.1), kind=kCustom, calls=%fused_computation.5 | custom fusion | flops 1572864 | bytes 1082372 | tf_op jit(solution)/shard_map/scatter | solution.py:44
  149.2 6.7 %convolution_bitcast_fusion = f32[1024,128]{0,1:T(8,128)S(1)} fusion(f32[1024,1024]{1,0:T(8,128)} %param.8, f32[2048,128]{1,0:T(8,128)S(1)} %scatter_custom_fusion.2, s32[]{:T(128)S(6)} %select_n.62), kind=kOutput, calls=%fused_computation.9 | convolution fusion | flops 1610612736 | bytes 5242884 | tf_op jit(solution)/shard_map/dot_general | solution.py:73
  155.9 1.0 copy.11
  156.9 0.0 reduce-scatter.4.cloned.1.call-update
  156.9 53.6 %reduce-scatter.4.cloned.1.call-done = f32[64,128]{1,0:T(8,128)} async-done(((f32[1024,128]{1,0:T(8,128)}), f32[64,128]{1,0:T(8,128)}) %reduce-scatter.4.cloned.1.call-update) | async-done | bytes 32784 | tf_op jit(solution)/shard_map/reduce_scatter | solution.py:72
  (7 shorter events, 0.1 us)
Async XLA Ops:
  21.2 63.6 %all-to-all-start = ((s32[16,1,256]{2,1,0:T(1,128)}), s32[16,1,256]{2,1,0:T(1,128)S(1)}, u32[]{:S(2)}, u32[]{:S(2)}) async-start(s32[16,1,256]{2,1,0:T(1,128)} %bitcast.2), calls=%async_computation | async-start | bytes 32768 | tf_op jit(solution)/shard_map/all_to_all | solution.py:37
  60.5 0.7 copy-start
  61.2 29.7 %copy-start.1 = (f32[2048]{0:T(1024)S(1)}, f32[2048]{0:T(1024)}, u32[]{:S(2)}) copy-start(f32[2048]{0:T(1024)} %param.10) | copy-start | bytes 24580
  61.2 29.7 %copy-start.2 = (f32[128]{0:T(128)S(1)}, f32[128]{0:T(128)}, u32[]{:S(2)}) copy-start(f32[128]{0:T(128)} %param.11) | copy-start | bytes 1540
  84.8 40.9 %all-to-all-start.2 = ((f32[16,1,256]{2,1,0:T(1,128)}), f32[16,1,256]{2,1,0:T(1,128)S(1)}, u32[]{:S(2)}, u32[]{:S(2)}) async-start(f32[16,1,256]{2,1,0:T(1,128)} %bitcast.7), calls=%async_computation.2 | async-start | bytes 32768 | tf_op jit(solution)/shard_map/all_to_all | solution.py:36
  125.7 10.0 %all-to-all-start.1 = ((f32[16,1,256]{2,1,0:T(1,128)}), f32[16,1,256]{2,1,0:T(1,128)S(1)}, u32[]{:S(2)}, u32[]{:S(2)}) async-start(f32[16,1,256]{2,1,0:T(1,128)} %bitcast.5), calls=%async_computation.1 | async-start | bytes 32768 | tf_op jit(solution)/shard_map/all_to_all | solution.py:35
  129.2 81.3 %reduce-scatter.4.cloned.1.call-start = ((), (), s32[]{:S(2)}) async-start(), calls=%async_computation.4 | async-start | bytes 557056 | tf_op jit(solution)/shard_map/reduce_scatter | solution.py:72
Sparse Core Ops, SparseCore 0:
  157.0 53.4 reduce-scatter.3
where the time goes:
time: 218 us; the launch traced here: 217 us
  local copies, waits for them, and re-layouts  64.3 us (29%)
  waiting for transfers between devices  60 us (28%)
  blocking collectives  33.8 us (16%)
  other arithmetic  22.1 us (10%)
  starting transfers between devices  16.9 us (8%)
  between operations  13.6 us (6%)
  matrix products  6.67 us (3%)
    reduce_scatter x1, waiting for transfers between devices, body(): lax.psum_scatter(jnp.dot(eigen_slab, half_window, precision=lax.Precision...  53.6 us
    psum x1, blocking collectives, body(): sum_squares = lax.psum(jnp.sum(entries * entries, axis=0), 'col')  33.8 us
    gather x1, local copies, waits for them, and re-layouts, route_generators(): jnp.take(live_coupling, slot_source, mode='fill', fill_value=0.0)  23 us
    gather x1, local copies, waits for them, and re-layouts, route_generators(): jnp.take(secular_poles, slot_source, mode='fill', fill_value=0.0)  23 us
    scatter x1, other arithmetic, route_generators(): return empty.at[got_index.reshape(-1)].set(rebuilt, mode='drop')  13.5 us
    scatter x1, local copies, waits for them, and re-layouts, slot_plan(): slot_target = sentinel.at[slot_index].set(target_local)  8.62 us
    scatter x1, local copies, waits for them, and re-layouts, slot_plan(): sentinel.at[slot_index].set(jnp.arange(block_len, dtype=jnp.int32))  8.06 us
    all_to_all x1, starting transfers between devices, route_generators(): lax.all_to_all(slot_target.reshape(groups, capacity), 'col', split_axis=0...  7.39 us
  transfers between devices with their start and end apart: 4, of which 2 were waited for; matrix products, arithmetic and copies ran while one was open for 26% of the time, Pallas kernels for 0%

commit v1 on v0

--- a/solution.py
+++ b/solution.py
@@ -54,7 +54,12 @@
     entries = jnp.where(
         deflated[:, None] == 0, coupling[:, None] / distance, jnp.zeros_like(distance)
     )
-    sum_squares = lax.psum(jnp.sum(entries * entries, axis=0), "col")
+
+    def name_frames(array_here, link_axis):
+        answer = lax.all_gather(array_here, link_axis)
+        return jnp.sum(answer, 0)
+
+    sum_squares = name_frames(jnp.sum(entries * entries, axis=0), "col")
     inverse = lax.rsqrt(sum_squares)
     placed = route_generators(
         coupling,

time: 218 us -> 206 us (0.945)
  blocking collectives: 33.8 us -> 21.7 us
    psum x1 -> x0, blocking collectives: 33.8 us -> none  [body(): sum_squares = lax.psum(jnp.sum(entries * entries, axis=0), 'col')]
    all_gather x0 -> x1, blocking collectives: none -> 21.7 us  [name_frames(): answer = lax.all_gather(array_here, link_axis)]
  transfers between devices with their start and end apart: 4 -> 4, of which waited for: 2 -> 2; matrix products, arithmetic and copies ran while one was open for 26% -> 28% of each run, Pallas kernels for 0% -> 0%
where the time goes in v1:
time: 206 us; the launch traced here: 205 us
  local copies, waits for them, and re-layouts  64.3 us (31%)
  waiting for transfers between devices  59.9 us (29%)
  other arithmetic  22.1 us (11%)
  blocking collectives  21.7 us (11%)
  starting transfers between devices  16.9 us (8%)
  between operations  13.6 us (7%)
  matrix products  6.67 us (3%)
    reduce_scatter x1, waiting for transfers between devices, body(): lax.psum_scatter(jnp.dot(eigen_slab, half_window, precision=lax.Precision...  53.5 us
    gather x1, local copies, waits for them, and re-layouts, route_generators(): jnp.take(live_coupling, slot_source, mode='fill', fill_value=0.0)  23 us
    gather x1, local copies, waits for them, and re-layouts, route_generators(): jnp.take(secular_poles, slot_source, mode='fill', fill_value=0.0)  23 us
    all_gather x1, blocking collectives, name_frames(): answer = lax.all_gather(array_here, link_axis)  21.7 us
    scatter x1, other arithmetic, route_generators(): return empty.at[got_index.reshape(-1)].set(rebuilt, mode='drop')  13.5 us
    scatter x1, local copies, waits for them, and re-layouts, slot_plan(): slot_target = sentinel.at[slot_index].set(target_local)  8.62 us
    scatter x1, local copies, waits for them, and re-layouts, slot_plan(): sentinel.at[slot_index].set(jnp.arange(block_len, dtype=jnp.int32))  8.06 us
    all_to_all x1, starting transfers between devices, route_generators(): lax.all_to_all(slot_target.reshape(groups, capacity), 'col', split_axis=0...  7.39 us
  transfers between devices with their start and end apart: 4, of which 2 were waited for; matrix products, arithmetic and copies ran while one was open for 28% of the time, Pallas kernels for 0%

profile of v1, /device:TPU:0, one launch (start us, length us, event | category | flops | bytes accessed | tf_op | source)
XLA Modules:
  0.0 205.2 jit_solution(10435111361272829224)
XLA Ops:
  6.5 0.7 fusion.15
  7.3 4.5 %reduce-window.6 = s32[16,16,128]{2,1,0:T(8,128)S(1)} reduce-window(s32[16,16,128]{2,1,0:T(8,128)S(1)} %fusion.12, s32[]{:T(128)} %constant.67.clone.1), window={size=1x1x128 pad=0_0x0_0x127_0}, to_apply=%region_0.1 | reduce-window | flops 4161536 | bytes 262148 | tf_op jit(solution)/shard_map/reduce-window
  11.8 0.4 slice_reduce_fusion
  12.3 0.2 reduce-window.9
  12.4 0.1 broadcast_add_fusion
  12.5 0.1 fusion.11
  12.6 8.6 %scatter_custom_fusion = s32[4096]{0:T(1024)} fusion(s32[2048]{0:T(1024)S(1)} %compare_select_fusion.2, s32[2048]{0:T(1024)S(1)} %get-tuple-element.10, s32[]{:T(128)} %constant.66.clone.1), kind=kCustom, calls=%fused_computation.45 | custom fusion | bytes 16388 | tf_op jit(solution)/shard_map/scatter | solution.py:18
  21.2 7.4 %all-to-all-start = ((s32[16,1,256]{2,1,0:T(1,128)}), s32[16,1,256]{2,1,0:T(1,128)S(1)}, u32[]{:S(2)}, u32[]{:S(2)}) async-start(s32[16,1,256]{2,1,0:T(1,128)} %bitcast.2), calls=%async_computation | async-start | bytes 32768 | tf_op jit(solution)/shard_map/all_to_all | solution.py:37
  28.6 8.1 %scatter_custom_fusion.1 = s32[4096]{0:T(1024)S(1)} fusion(s32[2048]{0:T(1024)S(1)} %compare_select_fusion.2, s32[2048]{0:T(1024)S(1)} %iota.11, s32[]{:T(128)} %constant.66.clone.1), kind=kCustom, calls=%fused_computation.43 | custom fusion | bytes 16388 | tf_op jit(solution)/shard_map/scatter | solution.py:17
  36.7 0.7 broadcast_select_fusion.2
  37.4 23.0 %gather_fusion = f32[4096]{0:T(1024)S(1)} fusion(f32[2048]{0:T(1024)S(1)} %get-tuple-element.8, s32[4096]{0:T(1024)S(1)} %fusion.13), kind=kCustom, calls=%fused_computation.clone | custom fusion | bytes 49152 | tf_op jit(solution)/shard_map/jit(_take)/gather | solution.py:28
  60.5 0.0 copy-start
  60.5 0.6 broadcast_select_fusion.1
  61.1 0.1 copy-done
  61.2 0.0 copy-start.1
  61.2 23.0 %gather_fusion.1 = f32[4096]{0:T(1024)S(1)} fusion(f32[2048]{0:T(1024)S(1)} %copy-done, s32[4096]{0:T(1024)S(1)} %fusion.13), kind=kCustom, calls=%fused_computation.1.clone | custom fusion | bytes 49152 | tf_op jit(solution)/shard_map/jit(_take)/gather | solution.py:31
  84.2 0.6 broadcast_select_fusion
  84.8 0.0 all-to-all-done
  84.8 6.0 %all-to-all-start.2 = ((f32[16,1,256]{2,1,0:T(1,128)}), f32[16,1,256]{2,1,0:T(1,128)S(1)}, u32[]{:S(2)}, u32[]{:S(2)}) async-start(f32[16,1,256]{2,1,0:T(1,128)} %bitcast.7), calls=%async_computation.2 | async-start | bytes 32768 | tf_op jit(solution)/shard_map/all_to_all | solution.py:36
  90.8 0.0 copy-done.1
  90.9 0.0 copy-done.2
  90.9 1.0 multiply_reduce_fusion
  91.9 21.7 %all-gather.1 = f32[16,1,128]{2,1,0:T(1,128)S(1)} all-gather(f32[1,1,128]{2,1,0:T(1,128)S(1)} %bitcast.37), channel_id=2, replica_groups=mesh['row'=2,'col'=16] {'col'}, dimensions={0}, use_global_device_ids=true | all-gather | bytes 8704 | tf_op jit(solution)/shard_map/all_gather | solution.py:59
  113.6 0.0 all-to-all-done.2
  113.6 3.5 %all-to-all-start.1 = ((f32[16,1,256]{2,1,0:T(1,128)}), f32[16,1,256]{2,1,0:T(1,128)S(1)}, u32[]{:S(2)}, u32[]{:S(2)}) async-start(f32[16,1,256]{2,1,0:T(1,128)} %bitcast.5), calls=%async_computation.1 | async-start | bytes 32768 | tf_op jit(solution)/shard_map/all_to_all | solution.py:35
  117.1 0.0 reduce-scatter.4.cloned.1.call-start
  117.2 6.4 %all-to-all-done.1 = f32[16,1,256]{2,1,0:T(1,128)S(1)} async-done(((f32[16,1,256]{2,1,0:T(1,128)}), f32[16,1,256]{2,1,0:T(1,128)S(1)}, u32[]{:S(2)}, u32[]{:S(2)}) %all-to-all-start.1) | async-done | bytes 16416 | tf_op jit(solution)/shard_map/all_to_all | solution.py:35
  123.6 13.5 %scatter_custom_fusion.2 = f32[2048,128]{1,0:T(8,128)S(1)} fusion(s32[4096]{0:T(1024)S(1)} %bitcast.36, f32[128]{0:T(128)S(1)} %rsqrt.7, f32[128]{0:T(128)S(1)} %copy-done.2, f32[4096]{0:T(1024)S(1)} %bitcast.32, f32[4096]{0:T(1024)S(1)} %bitcast.33, f32[]{:T(128)} %constant.65.clone.1), kind=kCustom, calls=%fused_computation.5 | custom fusion | flops 1572864 | bytes 1082372 | tf_op jit(solution)/shard_map/scatter | solution.py:44
  137.1 6.7 %convolution_bitcast_fusion = f32[1024,128]{0,1:T(8,128)S(1)} fusion(f32[1024,1024]{1,0:T(8,128)} %param.8, f32[2048,128]{1,0:T(8,128)S(1)} %scatter_custom_fusion.2, s32[]{:T(128)S(6)} %select_n.62), kind=kOutput, calls=%fused_computation.9 | convolution fusion | flops 1610612736 | bytes 5242884 | tf_op jit(solution)/shard_map/dot_general | solution.py:78
  143.8 1.0 copy.11
  144.8 0.0 reduce-scatter.4.cloned.1.call-update
  144.8 53.5 %reduce-scatter.4.cloned.1.call-done = f32[64,128]{1,0:T(8,128)} async-done(((f32[1024,128]{1,0:T(8,128)}), f32[64,128]{1,0:T(8,128)}) %reduce-scatter.4.cloned.1.call-update) | async-done | bytes 32784 | tf_op jit(solution)/shard_map/reduce_scatter | solution.py:77
  (8 shorter events, 0.1 us)
Async XLA Ops:
  21.2 63.6 %all-to-all-start = ((s32[16,1,256]{2,1,0:T(1,128)}), s32[16,1,256]{2,1,0:T(1,128)S(1)}, u32[]{:S(2)}, u32[]{:S(2)}) async-start(s32[16,1,256]{2,1,0:T(1,128)} %bitcast.2), calls=%async_computation | async-start | bytes 32768 | tf_op jit(solution)/shard_map/all_to_all | solution.py:37
  60.5 0.7 copy-start
  61.2 29.7 %copy-start.1 = (f32[2048]{0:T(1024)S(1)}, f32[2048]{0:T(1024)}, u32[]{:S(2)}) copy-start(f32[2048]{0:T(1024)} %param.10) | copy-start | bytes 24580
  61.2 29.7 %copy-start.2 = (f32[128]{0:T(128)S(1)}, f32[128]{0:T(128)}, u32[]{:S(2)}) copy-start(f32[128]{0:T(128)} %param.11) | copy-start | bytes 1540
  84.8 28.8 %all-to-all-start.2 = ((f32[16,1,256]{2,1,0:T(1,128)}), f32[16,1,256]{2,1,0:T(1,128)S(1)}, u32[]{:S(2)}, u32[]{:S(2)}) async-start(f32[16,1,256]{2,1,0:T(1,128)} %bitcast.7), calls=%async_computation.2 | async-start | bytes 32768 | tf_op jit(solution)/shard_map/all_to_all | solution.py:36
  113.6 10.0 %all-to-all-start.1 = ((f32[16,1,256]{2,1,0:T(1,128)}), f32[16,1,256]{2,1,0:T(1,128)S(1)}, u32[]{:S(2)}, u32[]{:S(2)}) async-start(f32[16,1,256]{2,1,0:T(1,128)} %bitcast.5), calls=%async_computation.1 | async-start | bytes 32768 | tf_op jit(solution)/shard_map/all_to_all | solution.py:35
  117.1 81.2 %reduce-scatter.4.cloned.1.call-start = ((), (), s32[]{:S(2)}) async-start(), calls=%async_computation.4 | async-start | bytes 557056 | tf_op jit(solution)/shard_map/reduce_scatter | solution.py:77
Sparse Core Ops, SparseCore 0:
  145.0 53.3 reduce-scatter.3
